TPU v7x, 32 devices: a whole 2x2x4 slice. The times are simulated.
32 devices in a mesh: freq: 4 (over y, x), panel: 8 (over z, core).
Axes of the slice: x: 2, y: 2, z: 4, core: 2. Of those that a mesh axis runs over, the one named last changes fastest.
Arguments:
- traces: bfloat16 [640, 640, 1024], P('panel', 'freq'), may hold values from -6 to 6
- filters: float32 [16, 7, 64], replicated, may hold values from -0.25 to 0.25
Outputs:
- primaries: bfloat16 [640, 640, 1024], P('panel', 'freq')
All inputs are finite; a program needn't handle non-finite values.
Results may differ from a plain program's by a relative error of at most 0.0095.
Values may be sent and summed in bfloat16 or wider, within the bound.
A program may use at most 192 MiB of HBM per device.

v0:
```python
import math

import jax
import jax.numpy as jnp
from jax import lax
from jax.sharding import PartitionSpec as P

NS = 640
NT = 1024
NF = 96
FLO = 8
TAPS = 64
SPAN = 7
RWIN = 40


def wave_table(freq_bins, sample_index):
    phases = freq_bins[:, None] * sample_index[None, :] % NT
    angles = phases.astype(jnp.float32) * jnp.float32(2.0 * math.pi / NT)
    return (jnp.cos(angles), jnp.sin(angles))


def complex_product(left_side, right_side):

    def factor_product(leading_factor, trailing_factor):
        return jnp.einsum(
            "gjo,god->gjd", leading_factor, trailing_factor, preferred_element_type=jnp.float32
        )

    part_real = factor_product(left_side[0], right_side[0]) - factor_product(
        left_side[1], right_side[1]
    )
    part_imag = factor_product(left_side[0], right_side[1]) + factor_product(
        left_side[1], right_side[0]
    )
    return jnp.stack([part_real, part_imag])


def response(filters, freq_bins):
    tap_index = jnp.arange(TAPS, dtype=jnp.int32)
    cosine_wave, sine_wave = wave_table(freq_bins, tap_index)
    filter_real = jnp.einsum("fk,wjk->fjw", cosine_wave, filters, precision=lax.Precision.HIGHEST)
    filter_imag = -jnp.einsum("fk,wjk->fjw", sine_wave, filters, precision=lax.Precision.HIGHEST)
    return (jnp.repeat(filter_real, RWIN, axis=2), jnp.repeat(filter_imag, RWIN, axis=2))


def apply_filter(extended, filter_real, filter_imag, source_count):
    sum_real = jnp.zeros(extended.shape[1:2] + (source_count,) + extended.shape[3:], jnp.float32)
    sum_imag = jnp.zeros_like(sum_real)
    for shifted in range(SPAN):
        part_real = extended[0, :, shifted : shifted + source_count, :]
        part_imag = extended[1, :, shifted : shifted + source_count, :]
        weight_real = filter_real[:, shifted][:, None, :]
        weight_imaginary = filter_imag[:, shifted][:, None, :]
        sum_real = sum_real + weight_real * part_real - weight_imaginary * part_imag
        sum_imag = sum_imag + weight_real * part_imag + weight_imaginary * part_real
    return jnp.stack([sum_real, sum_imag])


def per_device(traces, filters):
    shot_rows, receiver_cols, time_sample_count = traces.shape
    rim_width = SPAN // 2
    scale_sources = jnp.float32(math.sqrt(NS))
    freq_bins = FLO + jnp.arange(NF, dtype=jnp.int32)
    cosine_wave, sine_wave = wave_table(freq_bins, jnp.arange(NT, dtype=jnp.int32))
    forward = (jnp.concatenate([cosine_wave, -sine_wave], 0) / jnp.float32(math.sqrt(NT))).astype(
        jnp.bfloat16
    )
    reciprocal_value = jnp.concatenate([cosine_wave, -sine_wave], 0).astype(jnp.bfloat16)
    spectra = jnp.einsum("srt,ct->csr", traces, forward, preferred_element_type=jnp.float32)
    spectra = spectra.astype(jnp.bfloat16).reshape(2, NF, shot_rows, receiver_cols)
    columns = lax.all_to_all(spectra, "panel", split_axis=1, concat_axis=2, tiled=True)
    slice_count = columns.shape[1]
    first_slice = lax.axis_index("panel") * slice_count
    complete = lax.all_gather(columns, "freq", axis=3, tiled=True)
    order_one = (complex_product(complete, columns) / scale_sources).astype(jnp.bfloat16)
    order_two = complex_product(complete, order_one) / scale_sources
    prediction = (order_one.astype(jnp.float32) - order_two).astype(jnp.bfloat16)
    extended = jnp.pad(
        prediction.astype(jnp.float32), ((0, 0), (0, 0), (rim_width, rim_width), (0, 0))
    )
    own_bins = FLO + first_slice + jnp.arange(slice_count, dtype=jnp.int32)
    filter_real, filter_imag = response(filters, own_bins)
    receiver_start = lax.axis_index("freq") * receiver_cols
    filter_real = lax.dynamic_slice_in_dim(filter_real, receiver_start, receiver_cols, 2)
    filter_imag = lax.dynamic_slice_in_dim(filter_imag, receiver_start, receiver_cols, 2)
    matched = apply_filter(extended, filter_real, filter_imag, NS)
    returned = lax.all_to_all(
        matched.astype(jnp.bfloat16), "panel", split_axis=2, concat_axis=1, tiled=True
    )
    matched_rows = returned.reshape(2 * NF, shot_rows, receiver_cols)
    multiples = jnp.einsum(
        "csr,ct->srt", matched_rows, reciprocal_value, preferred_element_type=jnp.float32
    )
    multiples = multiples / jnp.float32(math.sqrt(NF))
    return (traces.astype(jnp.float32) - multiples).astype(jnp.bfloat16)


def solution(mesh):
    placed = (P("panel", "freq", None), P())
    return jax.shard_map(
        per_device, mesh=mesh, in_specs=placed, out_specs=P("panel", "freq", None), check_vma=False
    )
```

profile of v0, /device:TPU:0, one launch (start us, length us, event | category | flops | bytes accessed | tf_op | source)
XLA Modules:
  0.0 941.7 jit_solution(9572457835950158956)
XLA Ops:
  6.5 0.0 copy-start
  6.5 0.0 all-gather.2.cloned.1.call-start
  6.5 1.6 fusion.42
  8.2 0.0 copy-start.3
  8.2 0.0 copy-start.5
  8.2 0.7 copy-done.3
  8.9 0.2 copy-done.5
  9.1 13.8 %convolution_convert_fusion = bf16[192,80,160]{0,2,1:T(8,128)(2,1)} fusion(bf16[80,160,1024]{2,1,0:T(8,128)(2,1)} %param.2, f32[96,1024]{1,0:T(8,128)S(1)} %get-tuple-element.24, f32[96,1024]{1,0:T(8,128)S(1)} %get-tuple-element.23), kind=kOutput, calls=%fused_computation.35 | convolution fusion | flops 5036212224 | bytes 31916032 | tf_op jit(solution)/shard_map/srt,ct->csr/dot_general | solution.py:70
  22.9 15.0 %reshape.26 = bf16[2,96,80,160]{1,0,3,2:T(2,128)(2,1)} reshape(bf16[192,80,160]{0,2,1:T(8,128)(2,1)} %convolution_convert_fusion) | data formatting | bytes 9830400 | tf_op jit(solution)/shard_map/reshape | solution.py:71
  37.9 17.3 %copy.39 = bf16[2,96,80,160]{3,2,0,1:T(8,128)(2,1)} copy(bf16[2,96,80,160]{1,0,3,2:T(2,128)(2,1)} %reshape.26) | data formatting | bytes 9830400 | tf_op jit(solution)/shard_map/reshape | solution.py:71
  55.2 179.3 %all_to_all.33 = bf16[2,96,80,160]{3,2,0,1:T(8,128)(2,1)} all-to-all(bf16[2,96,80,160]{3,2,0,1:T(8,128)(2,1)} %copy.39), channel_id=1, replica_groups=mesh['freq'=4,'panel'=8] {'panel'}, dimensions={1} | all-to-all | bytes 9830400 | tf_op jit(solution)/shard_map/all_to_all | solution.py:72
  234.5 12.6 %copy.52 = bf16[2,12,8,80,160]{3,2,0,1,4:T(8,128)(2,1)} copy(bf16[2,12,8,80,160]{4,3,0,1,2:T(8,128)(2,1)} %bitcast.133) | data formatting | bytes 9830400 | tf_op jit(solution)/shard_map/all_to_all | solution.py:72
  247.1 16.3 %reshape.33 = bf16[2,12,640,160]{2,0,1,3:T(2,128)(2,1)} reshape(bf16[2,12,8,80,160]{3,2,0,1,4:T(8,128)(2,1)} %copy.52) | data formatting | bytes 9830400 | tf_op jit(solution)/shard_map/all_to_all | solution.py:72
  263.4 0.0 all-gather.2.cloned.1.call-update
  263.5 0.0 copy-done
  263.5 0.6 fusion.29
  264.1 0.6 convolution_bitcast_fusion
  264.7 0.2 broadcast_in_dim.4
  264.9 0.4 reshape.25
  265.3 0.2 broadcast_in_dim.5
  265.6 0.4 reshape.27
  266.0 0.5 constant_dynamic-slice_fusion.10
  266.6 0.6 copy.99
  267.2 4.5 copy.40
  271.7 4.5 fusion.67
  276.2 6.7 copy.46
  282.9 5.5 squeeze.15
  288.4 6.4 copy.44
  294.8 6.6 squeeze.13
  301.4 144.0 %all-gather.2.cloned.1.call-done = bf16[2,12,640,640]{2,0,1,3:T(2,128)(2,1)} async-done(((bf16[2,12,640,160]{2,0,1,3:T(2,128)(2,1)}), bf16[2,12,640,640]{2,0,1,3:T(2,128)(2,1)}) %all-gather.2.cloned.1.call-update) | async-done | bytes 19660816 | tf_op jit(solution)/shard_map/all_gather | solution.py:75
  445.4 38.6 %fusion.66 = (bf16[1,12,640,640]{2,0,1,3:T(2,128)(2,1)}, bf16[1,12,640,640]{2,0,1,3:T(2,128)(2,1)}) fusion(bf16[2,12,640,640]{2,0,1,3:T(2,128)(2,1)} %all-gather.2.cloned.1.call-done), kind=kLoop, calls=%fused_computation.120 | loop fusion | bytes 39321600 | tf_op jit(solution)/shard_map/slice | solution.py:30
  484.1 38.2 %copy.68 = bf16[1,12,640,640]{3,2,1,0:T(8,128)(2,1)} copy(bf16[1,12,640,640]{2,0,1,3:T(2,128)(2,1)} %get-tuple-element.5) | data formatting | bytes 19660800
  522.3 38.6 %copy.69 = bf16[1,12,640,640]{3,2,1,0:T(8,128)(2,1)} copy(bf16[1,12,640,640]{2,0,1,3:T(2,128)(2,1)} %get-tuple-element.6) | data formatting | bytes 19660800
  560.9 10.0 %fusion.7 = f32[12,640,160]{1,2,0:T(8,128)} fusion(bf16[12,640,160]{1,2,0:T(8,128)(2,1)} %squeeze.13, bf16[1,12,640,640]{3,2,1,0:T(8,128)(2,1)} %copy.69), kind=kOutput, calls=%fused_computation.22 | convolution fusion | flops 1572864000 | bytes 17203200 | tf_op jit(solution)/shard_map/gjo,god->gjd/dot_general | solution.py:26
  570.9 9.3 fusion.9
  580.2 10.8 %add_bitcast_fusion.1 = f32[1,12,640,160]{2,3,1,0:T(8,128)} fusion(f32[12,640,160]{1,2,0:T(8,128)} %fusion.7, bf16[12,640,160]{1,2,0:T(8,128)(2,1)S(1)} %squeeze.15, bf16[1,12,640,640]{3,2,1,0:T(8,128)(2,1)} %copy.68), kind=kOutput, calls=%fused_computation.42 | convolution fusion | flops 1574092800 | bytes 22118400 | tf_op jit(solution)/shard_map/gjo,god->gjd/dot_general | solution.py:26
  591.0 11.4 %subtract_bitcast_fusion.1 = f32[1,12,640,160]{2,3,1,0:T(8,128)} fusion(f32[12,640,160]{1,2,0:T(8,128)} %fusion.9, bf16[12,640,160]{1,2,0:T(8,128)(2,1)} %squeeze.13, bf16[1,12,640,640]{3,2,1,0:T(8,128)(2,1)} %copy.68), kind=kOutput, calls=%fused_computation.43 | convolution fusion | flops 1574092800 | bytes 22118400 | tf_op jit(solution)/shard_map/gjo,god->gjd/dot_general | solution.py:26
  602.5 5.1 fusion
  607.6 0.0 copy-start.2
  607.6 11.4 %fusion.3 = f32[12,640,160]{1,2,0:T(8,128)} fusion(bf16[1,12,640,640]{3,2,1,0:T(8,128)(2,1)} %copy.69, bf16[2,12,640,160]{2,3,1,0:T(8,128)(2,1)S(1)} %fusion), kind=kOutput, calls=%fused_computation.18 | convolution fusion | flops 1572864000 | bytes 17203200 | tf_op jit(solution)/shard_map/gjo,god->gjd/dot_general | solution.py:26
  618.9 0.0 copy-done.2
  618.9 9.3 fusion.5
  628.3 11.5 %subtract_bitcast_fusion = f32[1,12,640,160]{2,3,1,0:T(8,128)} fusion(f32[12,640,160]{1,2,0:T(8,128)} %fusion.5, bf16[1,12,640,640]{3,2,1,0:T(8,128)(2,1)} %copy.68, bf16[2,12,640,160]{2,3,1,0:T(8,128)(2,1)} %copy-done.2), kind=kOutput, calls=%fused_computation.41 | convolution fusion | flops 1574092800 | bytes 22118400 | tf_op jit(solution)/shard_map/gjo,god->gjd/dot_general | solution.py:26
  639.7 11.5 %add_bitcast_fusion = f32[1,12,640,160]{2,3,1,0:T(8,128)} fusion(f32[12,640,160]{1,2,0:T(8,128)} %fusion.3, bf16[1,12,640,640]{3,2,1,0:T(8,128)(2,1)} %copy.68, bf16[2,12,640,160]{2,3,1,0:T(8,128)(2,1)} %copy-done.2), kind=kOutput, calls=%fused_computation.40 | convolution fusion | flops 1574092800 | bytes 22118400 | tf_op jit(solution)/shard_map/gjo,god->gjd/dot_general | solution.py:26
  651.2 0.0 copy-start.7
  651.2 7.4 fusion.20
  658.6 0.0 copy-done.7
  658.7 21.9 %add_convert_fusion = bf16[1,12,640,160]{2,3,1,0:T(8,128)(2,1)S(1)} fusion(f32[2,12,640,160]{2,3,1,0:T(8,128)S(1)} %fusion.20, f32[12,160]{1,0:T(8,128)S(1)} %bitcast.149, f32[12,160]{1,0:T(8,128)S(1)} %bitcast.151, f32[12,160]{1,0:T(8,128)S(1)} %bitcast.139, f32[12,160]{1,0:T(8,128)S(1)} %bitcast.161, f32[12,160]{1,0:T(8,128)S(1)} %bitcast.141, ...), kind=kLoop, calls=%fused_computation.38 | loop fusion | flops 34406400 | bytes 22347776 | tf_op jit(solution)/shard_map/convert.1
  680.5 21.9 %subtract_convert_fusion.1 = bf16[1,12,640,160]{2,3,1,0:T(8,128)(2,1)S(1)} fusion(f32[2,12,640,160]{2,3,1,0:T(8,128)S(1)} %fusion.20, f32[12,160]{1,0:T(8,128)S(1)} %bitcast.150, f32[12,160]{1,0:T(8,128)S(1)} %bitcast.152, f32[12,160]{1,0:T(8,128)S(1)} %bitcast.140, f32[12,160]{1,0:T(8,128)S(1)} %bitcast.162, f32[12,160]{1,0:T(8,128)S(1)} %bitcast.142, ...), kind=kLoop, calls=%fused_computation.39 | loop fusion | flops 34406400 | bytes 22347776 | tf_op jit(solution)/shard_map/convert
  702.4 2.7 pad_maximum_fusion
  705.1 19.4 %copy.48 = bf16[2,12,640,160]{3,0,1,2:T(2,128)(2,1)} copy(bf16[2,12,640,160]{2,3,1,0:T(8,128)(2,1)} %pad_maximum_fusion) | data formatting | bytes 9830400 | tf_op jit(solution)/shard_map/stack | solution.py:57
  724.6 177.2 %all_to_all.34 = bf16[2,12,640,160]{3,0,1,2:T(2,128)(2,1)S(1)} all-to-all(bf16[2,12,640,160]{3,0,1,2:T(2,128)(2,1)} %copy.48), channel_id=1, replica_groups=mesh['freq'=4,'panel'=8] {'panel'}, dimensions={2} | all-to-all | bytes 9830400 | tf_op jit(solution)/shard_map/all_to_all | solution.py:88
  901.8 0.0 copy-start.4
  901.8 0.0 copy-start.6
  901.8 4.9 copy.49
  906.7 0.0 copy-done.4
  906.7 0.0 copy-done.6
  906.7 0.0 copy-start.1
  906.7 27.9 %subtract_convert_fusion = bf16[80,160,1024]{2,1,0:T(8,128)(2,1)} fusion(bf16[80,160,1024]{2,1,0:T(8,128)(2,1)} %param.2, bf16[192,80,160]{2,1,0:T(8,128)(2,1)} %bitcast.136, f32[96,1024]{1,0:T(8,128)S(1)} %copy-done.6, f32[96,1024]{1,0:T(8,128)S(1)} %copy-done.4), kind=kOutput, calls=%fused_computation | convolution fusion | flops 5086380032 | bytes 58130432 | tf_op jit(solution)/shard_map/csr,ct->srt/dot_general | solution.py:92
  934.6 0.0 copy-done.1
  (17 shorter events, 0.1 us)
Async XLA Ops:
  6.5 256.9 %copy-start = (f32[16,7,64]{2,0,1:T(8,128)S(1)}, f32[16,7,64]{2,0,1:T(8,128)}, u32[]{:S(2)}) copy-start(f32[16,7,64]{2,0,1:T(8,128)} %param.3) | copy-start | bytes 86020
  6.5 438.9 %all-gather.2.cloned.1.call-start = ((), (), s32[]{:S(2)}) async-start(), calls=%async_computation.2 | async-start | bytes 24576000 | tf_op jit(solution)/shard_map/all_gather | solution.py:75
  8.2 0.7 copy-start.3
  8.2 0.9 copy-start.5
  607.6 11.4 %copy-start.2 = (bf16[2,12,640,160]{2,3,1,0:T(8,128)(2,1)}, bf16[2,12,640,160]{2,3,1,0:T(8,128)(2,1)S(1)}, u32[]{:S(2)}) copy-start(bf16[2,12,640,160]{2,3,1,0:T(8,128)(2,1)S(1)} %fusion) | copy-start | bytes 14745604
  651.2 7.4 copy-start.7
  901.8 4.9 copy-start.4
  901.8 4.9 copy-start.6
  906.7 27.9 %copy-start.1 = (f32[16,7,64]{2,0,1:T(8,128)S(1)}, f32[16,7,64]{2,0,1:T(8,128)}, u32[]{:S(2)}) copy-start(f32[16,7,64]{2,0,1:T(8,128)} %param.3) | copy-start | bytes 86020
Sparse Core Ops, SparseCore 0:
  263.6 181.7 all-gather.1
where the time goes:
time: 952 us; the launch traced here: 942 us
  blocking collectives  357 us (38%)
  local copies, waits for them, and re-layouts  239 us (25%)
  waiting for transfers between devices  144 us (15%)
  matrix products  128 us (13%)
  other arithmetic  60.6 us (6%)
  between operations  13.9 us (1%)
    all_to_all x1, blocking collectives, per_device(): lax.all_to_all(spectra, 'panel', split_axis=1, concat_axis=2, tiled=True)  179 us
    all_to_all x1, blocking collectives, per_device(): lax.all_to_all(matched.astype(jnp.bfloat16), 'panel', split_axis=2, conca...  177 us
    all_gather x1, waiting for transfers between devices, per_device(): complete = lax.all_gather(columns, 'freq', axis=3, tiled=True)  144 us
    dot_general x8, matrix products, factor_product(): jnp.einsum('gjo,god->gjd', leading_factor, trailing_factor, preferred_ele...  85.2 us
    unnamed x32, local copies, waits for them, and re-layouts  78.4 us
    another operation x2, other arithmetic  43.8 us
    slice x1, local copies, waits for them, and re-layouts, complex_product(): left_side[0]  38.6 us
    all_to_all x3, local copies, waits for them, and re-layouts, per_device(): lax.all_to_all(spectra, 'panel', split_axis=1, concat_axis=2, tiled=True)  33.4 us
  transfers between devices with their start and end apart: 1, of which 1 were waited for; matrix products, arithmetic and copies ran while one was open for 4% of the time, Pallas kernels for 0%

commit v1 on v0

--- a/solution.py
+++ b/solution.py
@@ -1,8 +1,11 @@
+import functools
 import math
 
 import jax
 import jax.numpy as jnp
 from jax import lax
+from jax.experimental import pallas as pl
+from jax.experimental.pallas import tpu as pltpu
 from jax.sharding import PartitionSpec as P
 
 NS = 640
@@ -12,28 +15,14 @@
 TAPS = 64
 SPAN = 7
 RWIN = 40
+LANES = 128
+AXES = ("panel", "freq")
 
 
 def wave_table(freq_bins, sample_index):
     phases = freq_bins[:, None] * sample_index[None, :] % NT
     angles = phases.astype(jnp.float32) * jnp.float32(2.0 * math.pi / NT)
     return (jnp.cos(angles), jnp.sin(angles))
-
-
-def complex_product(left_side, right_side):
-
-    def factor_product(leading_factor, trailing_factor):
-        return jnp.einsum(
-            "gjo,god->gjd", leading_factor, trailing_factor, preferred_element_type=jnp.float32
-        )
-
-    part_real = factor_product(left_side[0], right_side[0]) - factor_product(
-        left_side[1], right_side[1]
-    )
-    part_imag = factor_product(left_side[0], right_side[1]) + factor_product(
-        left_side[1], right_side[0]
-    )
-    return jnp.stack([part_real, part_imag])
 
 
 def response(filters, freq_bins):
@@ -42,6 +31,311 @@
     filter_real = jnp.einsum("fk,wjk->fjw", cosine_wave, filters, precision=lax.Precision.HIGHEST)
     filter_imag = -jnp.einsum("fk,wjk->fjw", sine_wave, filters, precision=lax.Precision.HIGHEST)
     return (jnp.repeat(filter_real, RWIN, axis=2), jnp.repeat(filter_imag, RWIN, axis=2))
+
+
+class Plan:
+    def __init__(self, shots, receivers, times, panels, columns):
+        self.shots, self.receivers, self.times = shots, receivers, times
+        self.panels, self.columns = panels, columns
+        self.devices = panels * columns
+        self.tail = receivers - LANES
+        self.fits = (
+            self.tail > 0
+            and LANES % self.tail == 0
+            and self.tail % 16 == 0
+            and columns * self.tail == LANES
+            and NF % self.devices == 0
+        )
+        if not self.fits:
+            return
+        self.fold = LANES // self.tail
+        self.group = shots // self.fold
+        self.fits = shots % 16 == 0 and shots % self.fold == 0 and self.group % 2 == 0
+        self.slices = NF // self.devices
+        self.rows = 2 * shots + 2 * self.group
+        self.fits = self.fits and self.rows % 8 == 0
+        self.side = NS
+        self.runs = []
+        for column in range(columns):
+            self.runs.append((column * receivers, column * LANES, LANES))
+        for column in range(columns):
+            self.runs.append(
+                (column * receivers + LANES, columns * LANES + column * self.tail, self.tail)
+            )
+
+    def cut(self, start, size):
+        parts = []
+        for natural, moved, length in self.runs:
+            low, high = max(start, natural), min(start + size, natural + length)
+            if low < high:
+                parts.append((low - start, moved + low - natural, high - low))
+        return parts
+
+
+def spectrum_kernel(plan, step_size, table_ref, traces_ref, out_ref, wide_ref):
+    step = pl.program_id(0)
+    fold, group, shots, times = plan.fold, plan.group, plan.shots, plan.times
+
+    def place(values, row, lane):
+        for part in range(2):
+            wide_ref[pl.ds(part * row[1] + row[0], NF, stride=plan.rows), :] = values[
+                part * NF : (part + 1) * NF, lane * LANES : (lane + 1) * LANES
+            ]
+
+    contract = (((1,), (1,)), ((), ()))
+    table = table_ref[...]
+    for a in range(fold):
+        main = traces_ref[a, :, :LANES, :].reshape(step_size * LANES, times)
+        values = lax.dot_general(table, main, contract, preferred_element_type=jnp.float32)
+        for j in range(step_size):
+            place(values, (a * group + step * step_size + j, shots), j)
+    tails = jnp.concatenate(
+        [
+            traces_ref[:, j, LANES:, :].reshape(fold * plan.tail, times)
+            for j in range(step_size)
+        ],
+        axis=0,
+    )
+    values = lax.dot_general(table, tails, contract, preferred_element_type=jnp.float32)
+    for j in range(step_size):
+        place(values, (2 * shots + step * step_size + j, group), j)
+
+    @pl.when(step == pl.num_programs(0) - 1)
+    def _():
+        @pl.loop(0, NF)
+        def _(f):
+            rows = pl.ds(pl.multiple_of(f * plan.rows, 8), plan.rows)
+            out_ref[rows, :] = wide_ref[rows, :].astype(jnp.bfloat16)
+
+
+def spectrum(plan, traces, table):
+    fold, group = plan.fold, plan.group
+    step_size = 2
+    shape = (NF * plan.rows, LANES)
+    return pl.pallas_call(
+        functools.partial(spectrum_kernel, plan, step_size),
+        grid=(group // step_size,),
+        out_shape=jax.ShapeDtypeStruct(shape, jnp.bfloat16),
+        in_specs=[
+            pl.BlockSpec(table.shape, lambda i: (0, 0)),
+            pl.BlockSpec((fold, step_size, plan.receivers, plan.times), lambda i: (0, i, 0, 0)),
+        ],
+        out_specs=pl.BlockSpec(shape, lambda i: (0, 0)),
+        scratch_shapes=[pltpu.VMEM(shape, jnp.float32)],
+        name="spectrum",
+    )(table, traces.reshape(fold, group, plan.receivers, plan.times))
+
+
+def inverse_kernel(plan, step_size, table_ref, matched_ref, traces_ref, out_ref, wide_ref):
+    step = pl.program_id(0)
+    fold, group, shots, times = plan.fold, plan.group, plan.shots, plan.times
+    scale = jnp.float32(1.0 / math.sqrt(NF))
+
+    @pl.when(step == 0)
+    def _():
+        @pl.loop(0, NF)
+        def _(f):
+            rows = pl.ds(pl.multiple_of(f * plan.rows, 8), plan.rows)
+            wide_ref[rows, :] = matched_ref[rows, :].astype(jnp.float32)
+
+    def fetch(row, spread):
+        parts = [
+            wide_ref[pl.ds(part * spread + row, NF, stride=plan.rows), :].T for part in range(2)
+        ]
+        return jnp.concatenate(parts, axis=1).astype(jnp.bfloat16)
+
+    table = table_ref[...]
+    for j in range(step_size):
+        for a in range(fold):
+            values = jnp.dot(
+                fetch(a * group + step * step_size + j, shots),
+                table,
+                preferred_element_type=jnp.float32,
+            )
+            own = traces_ref[a, j, :LANES, :].astype(jnp.float32)
+            out_ref[a, j, :LANES, :] = (own - values * scale).astype(jnp.bfloat16)
+        values = jnp.dot(
+            fetch(2 * shots + step * step_size + j, group),
+            table,
+            preferred_element_type=jnp.float32,
+        )
+        own = traces_ref[:, j, LANES:, :].astype(jnp.float32)
+        values = values.reshape(fold, plan.tail, times)
+        out_ref[:, j, LANES:, :] = (own - values * scale).astype(jnp.bfloat16)
+
+
+def subtract(plan, traces, matched, table):
+    fold, group = plan.fold, plan.group
+    step_size = 2
+    shape = (NF * plan.rows, LANES)
+    block = pl.BlockSpec((fold, step_size, plan.receivers, plan.times), lambda i: (0, i, 0, 0))
+    view = (fold, group, plan.receivers, plan.times)
+    out = pl.pallas_call(
+        functools.partial(inverse_kernel, plan, step_size),
+        grid=(group // step_size,),
+        out_shape=jax.ShapeDtypeStruct(view, jnp.bfloat16),
+        in_specs=[
+            pl.BlockSpec(table.shape, lambda i: (0, 0)),
+            pl.BlockSpec(shape, lambda i: (0, 0)),
+            block,
+        ],
+        out_specs=block,
+        scratch_shapes=[pltpu.VMEM(shape, jnp.float32)],
+        name="inverse",
+    )(table, matched, traces.reshape(view))
+    return out.reshape(traces.shape)
+
+
+RIM = 8
+CHUNK = 256
+
+
+def predict_kernel(
+    plan, weight_ref, in_ref, out_ref, left_ref, right_ref, first_ref, side_ref, ahead_ref, fold_ref
+):
+    shots, group, fold, tail = plan.shots, plan.group, plan.fold, plan.tail
+    side, columns, panels = plan.side, plan.columns, plan.panels
+    scale = jnp.float32(1.0 / math.sqrt(NS))
+    tails_at = columns * LANES
+
+    for panel in range(panels):
+        parts = plan.cut(panel * shots, shots)
+        for column in range(columns):
+            source = panel * columns + column
+            for part in range(2):
+                lanes = slice(part * side + column * LANES, part * side + (column + 1) * LANES)
+                for offset, row, length in parts:
+                    at = part * shots + offset
+                    left_ref[row : row + length, lanes] = in_ref[source, at : at + length, :]
+            packed = in_ref[source, 2 * shots :, :].astype(jnp.float32)
+            for part in range(2):
+                for a in range(fold):
+                    side_ref[
+                        part,
+                        panel * shots + a * group : panel * shots + (a + 1) * group,
+                        column * tail : (column + 1) * tail,
+                    ] = packed[part * group : (part + 1) * group, a * tail : (a + 1) * tail]
+    for natural, moved, length in plan.runs:
+        for part in range(2):
+            left_ref[
+                moved : moved + length, part * side + tails_at : (part + 1) * side
+            ] = side_ref[part, natural : natural + length, :].astype(jnp.bfloat16)
+
+    def fill(from_ref):
+        right_ref[:side, :] = from_ref[...]
+        right_ref[side:, :side] = -from_ref[:, side:]
+        right_ref[side:, side:] = from_ref[:, :side]
+
+    fill(left_ref)
+
+    @pl.loop(0, 2 * side // CHUNK)
+    def _(k):
+        lanes = pl.ds(pl.multiple_of(k * CHUNK, CHUNK), CHUNK)
+        total = jnp.dot(left_ref[...], right_ref[:, lanes], preferred_element_type=jnp.float32)
+        first_ref[:, lanes] = (total * scale).astype(jnp.bfloat16)
+
+    fill(first_ref)
+    ahead_ref[:RIM, :] = jnp.zeros((RIM, 2 * side), jnp.float32)
+    ahead_ref[RIM + side :, :] = jnp.zeros((RIM, 2 * side), jnp.float32)
+
+    @pl.loop(0, 2 * side // CHUNK)
+    def _(k):
+        lanes = pl.ds(pl.multiple_of(k * CHUNK, CHUNK), CHUNK)
+        total = jnp.dot(left_ref[...], right_ref[:, lanes], preferred_element_type=jnp.float32)
+        value = first_ref[:, lanes].astype(jnp.float32) - total * scale
+        value = value.astype(jnp.bfloat16).astype(jnp.float32)
+        for natural, moved, length in plan.runs:
+            ahead_ref[RIM + natural : RIM + natural + length, lanes] = value[moved : moved + length]
+
+    @pl.loop(0, panels)
+    def _(panel):
+        rows = pl.ds(pl.multiple_of(panel * shots, 8), shots + 2 * RIM)
+        for column in range(columns + 1):
+            at = column * LANES
+            real = ahead_ref[rows, at : at + LANES]
+            imag = ahead_ref[rows, side + at : side + at + LANES]
+            sum_real = sum_imag = None
+            for j in range(SPAN):
+                low = RIM - SPAN // 2 + j
+                part_real, part_imag = real[low : low + shots], imag[low : low + shots]
+                weight_real = weight_ref[0, j : j + 1, at : at + LANES]
+                weight_imag = weight_ref[1, j : j + 1, at : at + LANES]
+                term_real = weight_real * part_real - weight_imag * part_imag
+                term_imag = weight_real * part_imag + weight_imag * part_real
+                sum_real = term_real if j == 0 else sum_real + term_real
+                sum_imag = term_imag if j == 0 else sum_imag + term_imag
+            if column < columns:
+                target = panel * columns + column
+                out_ref[target, :shots, :] = sum_real.astype(jnp.bfloat16)
+                out_ref[target, shots : 2 * shots, :] = sum_imag.astype(jnp.bfloat16)
+                continue
+            for part, total in enumerate((sum_real, sum_imag)):
+                for other in range(columns):
+                    for a in range(fold):
+                        fold_ref[
+                            other,
+                            part * group : (part + 1) * group,
+                            a * tail : (a + 1) * tail,
+                        ] = total[a * group : (a + 1) * group, other * tail : (other + 1) * tail]
+            for other in range(columns):
+                out_ref[panel * columns + other, 2 * shots :, :] = fold_ref[other].astype(
+                    jnp.bfloat16
+                )
+
+
+def predict(plan, blocks, weights):
+    side = plan.side
+    block = pl.BlockSpec((plan.devices, plan.rows, LANES), lambda f: (0, f, 0))
+    return pl.pallas_call(
+        functools.partial(predict_kernel, plan),
+        grid=(plan.slices,),
+        out_shape=jax.ShapeDtypeStruct(blocks.shape, jnp.bfloat16),
+        in_specs=[pl.BlockSpec((None, 2, 8, side), lambda f: (f, 0, 0, 0)), block],
+        out_specs=block,
+        scratch_shapes=[
+            pltpu.VMEM((side, 2 * side), jnp.bfloat16),
+            pltpu.VMEM((2 * side, 2 * side), jnp.bfloat16),
+            pltpu.VMEM((side, 2 * side), jnp.bfloat16),
+            pltpu.VMEM((2, side, LANES), jnp.float32),
+            pltpu.VMEM((side + 2 * RIM, 2 * side), jnp.float32),
+            pltpu.VMEM((plan.columns, 2 * plan.group, LANES), jnp.float32),
+        ],
+        name="predict",
+    )(weights, blocks)
+
+
+def moved_lanes(plan, values):
+    split = values.reshape(values.shape[:-1] + (plan.columns, plan.receivers))
+    main = split[..., :LANES].reshape(values.shape[:-1] + (plan.columns * LANES,))
+    tail = split[..., LANES:].reshape(values.shape[:-1] + (plan.columns * plan.tail,))
+    return jnp.concatenate([main, tail], axis=-1)
+
+
+def per_device(plan, traces, filters):
+    freq_bins = FLO + jnp.arange(NF, dtype=jnp.int32)
+    cosine_wave, sine_wave = wave_table(freq_bins, jnp.arange(NT, dtype=jnp.int32))
+    waves = jnp.concatenate([cosine_wave, -sine_wave], 0)
+    forward = (waves / jnp.float32(math.sqrt(NT))).astype(jnp.bfloat16)
+    inverse = waves.astype(jnp.bfloat16)
+    wire = (plan.devices, plan.slices * plan.rows, LANES)
+
+    spectra = spectrum(plan, traces, forward).reshape(wire)
+    received = lax.all_to_all(spectra, AXES, split_axis=0, concat_axis=0, tiled=True)
+    own = lax.axis_index(AXES) * plan.slices + jnp.arange(plan.slices, dtype=jnp.int32)
+    weights = jnp.stack([moved_lanes(plan, w) for w in response(filters, FLO + own)], axis=1)
+    weights = jnp.pad(weights, ((0, 0), (0, 0), (0, 8 - SPAN), (0, 0)))
+    matched = predict(plan, received, weights)
+    returned = lax.all_to_all(matched, AXES, split_axis=0, concat_axis=0, tiled=True)
+    return subtract(plan, traces, returned.reshape(NF * plan.rows, LANES), inverse)
+
+
+def complex_product(left_side, right_side):
+    product = functools.partial(
+        jnp.einsum, "gjo,god->gjd", preferred_element_type=jnp.float32
+    )
+    part_real = product(left_side[0], right_side[0]) - product(left_side[1], right_side[1])
+    part_imag = product(left_side[0], right_side[1]) + product(left_side[1], right_side[0])
+    return jnp.stack([part_real, part_imag])
 
 
 def apply_filter(extended, filter_real, filter_imag, source_count):
@@ -57,16 +351,14 @@
     return jnp.stack([sum_real, sum_imag])
 
 
-def per_device(traces, filters):
+def per_device_general(traces, filters):
     shot_rows, receiver_cols, time_sample_count = traces.shape
     rim_width = SPAN // 2
     scale_sources = jnp.float32(math.sqrt(NS))
     freq_bins = FLO + jnp.arange(NF, dtype=jnp.int32)
     cosine_wave, sine_wave = wave_table(freq_bins, jnp.arange(NT, dtype=jnp.int32))
-    forward = (jnp.concatenate([cosine_wave, -sine_wave], 0) / jnp.float32(math.sqrt(NT))).astype(
-        jnp.bfloat16
-    )
-    reciprocal_value = jnp.concatenate([cosine_wave, -sine_wave], 0).astype(jnp.bfloat16)
+    waves = jnp.concatenate([cosine_wave, -sine_wave], 0)
+    forward = (waves / jnp.float32(math.sqrt(NT))).astype(jnp.bfloat16)
     spectra = jnp.einsum("srt,ct->csr", traces, forward, preferred_element_type=jnp.float32)
     spectra = spectra.astype(jnp.bfloat16).reshape(2, NF, shot_rows, receiver_cols)
     columns = lax.all_to_all(spectra, "panel", split_axis=1, concat_axis=2, tiled=True)
@@ -90,7 +382,7 @@
     )
     matched_rows = returned.reshape(2 * NF, shot_rows, receiver_cols)
     multiples = jnp.einsum(
-        "csr,ct->srt", matched_rows, reciprocal_value, preferred_element_type=jnp.float32
+        "csr,ct->srt", matched_rows, waves.astype(jnp.bfloat16), preferred_element_type=jnp.float32
     )
     multiples = multiples / jnp.float32(math.sqrt(NF))
     return (traces.astype(jnp.float32) - multiples).astype(jnp.bfloat16)
@@ -98,6 +390,15 @@
 
 def solution(mesh):
     placed = (P("panel", "freq", None), P())
+    panels, columns = mesh.shape["panel"], mesh.shape["freq"]
+
+    def body(traces, filters):
+        shots, receivers, times = traces.shape
+        plan = Plan(shots, receivers, times, panels, columns)
+        if plan.fits:
+            return per_device(plan, traces, filters)
+        return per_device_general(traces, filters)
+
     return jax.shard_map(
-        per_device, mesh=mesh, in_specs=placed, out_specs=P("panel", "freq", None), check_vma=False
-    )
+        body, mesh=mesh, in_specs=placed, out_specs=P("panel", "freq", None), check_vma=False
+    )

time: 952 us -> 326 us (0.34); the launches traced: 942 us -> 325 us
  blocking collectives: 357 us -> 0 us
  local copies, waits for them, and re-layouts: 239 us -> 0.75 us
  matrix products: 128 us -> 1.05 us
  Pallas kernels: 0 us -> 89 us
  waiting for transfers between devices: 144 us -> 217 us
  other arithmetic: 60.6 us -> 3.92 us
  between operations: 13.9 us -> 0.16 us
  starting transfers between devices: 0.01 us -> 13.5 us
    all_to_all x2 -> x0, blocking collectives: 357 us -> none  [the longest x1 179 us: per_device(): lax.all_to_all(spectra, 'panel', split_axis=1, concat_axis=2, tiled=True)]
    all_to_all x0 -> x2, waiting for transfers between devices: none -> 217 us  [the longest x1 109 us: per_device(): lax.all_to_all(matched, AXES, split_axis=0, concat_axis=0, tiled=True)]
    all_gather x1 -> x0, waiting for transfers between devices: 144 us -> none  [per_device(): complete = lax.all_gather(columns, 'freq', axis=3, tiled=True)]
    dot_general x10 -> x0, matrix products: 127 us -> none  [the longest x8 85.2 us: factor_product(): jnp.einsum('gjo,god->gjd', leading_factor, trailing_factor, preferred_ele...]
    pallas_call x0 -> x3, Pallas kernels: none -> 89 us  [the longest x1 42.9 us: predict(): pl.pallas_call(functools.partial(predict_kernel, plan), grid=(plan.slices...]
    unnamed x32 -> x4, local copies, waits for them, and re-layouts: 78.4 us -> 0.01 us
    slice x5 -> x4, local copies, waits for them, and re-layouts: 56.7 us -> 0.04 us  [the longest x2 0.02 us: moved_lanes(): split[..., :LANES].reshape(values.shape[:-1] + (plan.columns * LANES,))]
    another operation x3 -> x2, other arithmetic: 46.5 us -> 0.68 us  [per_device(): jnp.stack([moved_lanes(plan, w) for w in response(filters, FLO + own)], a...]
  transfers between devices with their start and end apart: 1 -> 2, of which waited for: 1 -> 2; matrix products, arithmetic and copies ran while one was open for 4% -> 1% of each run, Pallas kernels for 0% -> 0%
where the time goes in v1:
time: 326 us; the launch traced here: 325 us
  waiting for transfers between devices  217 us (67%)
  Pallas kernels  89 us (27%)
  starting transfers between devices  13.5 us (4%)
  other arithmetic  3.92 us (1%)
    all_to_all x1, waiting for transfers between devices, per_device(): lax.all_to_all(matched, AXES, split_axis=0, concat_axis=0, tiled=True)  109 us
    all_to_all x1, waiting for transfers between devices, per_device(): lax.all_to_all(spectra, AXES, split_axis=0, concat_axis=0, tiled=True)  108 us
    pallas_call x1, Pallas kernels, predict(): pl.pallas_call(functools.partial(predict_kernel, plan), grid=(plan.slices...  42.9 us
    pallas_call x1, Pallas kernels, subtract(): pl.pallas_call(functools.partial(inverse_kernel, plan, step_size), grid=(...  27.5 us
    pallas_call x1, Pallas kernels, spectrum(): pl.pallas_call(functools.partial(spectrum_kernel, plan, step_size), grid=...  18.6 us
    all_to_all x1, starting transfers between devices, per_device(): lax.all_to_all(spectra, AXES, split_axis=0, concat_axis=0, tiled=True)  7.44 us
  transfers between devices with their start and end apart: 2, of which 2 were waited for; matrix products, arithmetic and copies ran while one was open for 1% of the time, Pallas kernels for 0%

profile of v1, /device:TPU:0, one launch (start us, length us, event | category | flops | bytes accessed | tf_op | source)
XLA Modules:
  0.0 325.3 jit_solution(14380007772294302243)
XLA Ops:
  0.0 0.0 copy-start
  0.0 1.6 fusion.8
  1.6 0.8 multiply_convert_fusion.table_ref
  2.4 18.6 %spectrum.1 = bf16[19200,128]{1,0:T(8,128)(2,1)} custom-call(bf16[192,1024]{1,0:T(8,128)(2,1)} %multiply_convert_fusion.table_ref, bf16[4,20,160,1024]{3,2,1,0:T(8,128)(2,1)} %bitcast.24), custom_call_target="tpu_custom_call" | custom-call | tf_op jit(solution)/shard_map/spectrum/pallas_call | solution.py:115
  21.0 7.4 %all-to-all-start = ((bf16[32,600,128]{2,1,0:T(8,128)(2,1)}), bf16[32,600,128]{2,1,0:T(8,128)(2,1)}, u32[]{:S(2)}, u32[]{:S(2)}) async-start(bf16[32,600,128]{2,1,0:T(8,128)(2,1)} %bitcast.26), calls=%async_computation | async-start | bytes 9830400 | tf_op jit(solution)/shard_map/all_to_all | solution.py:323
  28.5 0.0 copy-done
  28.5 0.5 convolution_bitcast_fusion
  29.0 0.1 broadcast_in_dim.4
  29.1 0.1 reshape_reshape.6
  29.3 0.5 fusion
  29.9 0.1 broadcast_in_dim.5
  30.0 0.1 reshape_reshape.7
  30.1 0.1 reshape.35
  30.3 0.1 reshape.37
  30.4 0.7 select_maximum_fusion.weight_ref
  31.1 107.6 %all-to-all-done.in_ref = bf16[32,600,128]{2,1,0:T(8,128)(2,1)} async-done(((bf16[32,600,128]{2,1,0:T(8,128)(2,1)}), bf16[32,600,128]{2,1,0:T(8,128)(2,1)}, u32[]{:S(2)}, u32[]{:S(2)}) %all-to-all-start) | async-done | bytes 4915232 | tf_op jit(solution)/shard_map/all_to_all | solution.py:323
  138.7 42.9 %predict.1 = bf16[32,600,128]{2,1,0:T(8,128)(2,1)} custom-call(f32[3,2,8,640]{3,2,1,0:T(8,128)} %select_maximum_fusion.weight_ref, bf16[32,600,128]{2,1,0:T(8,128)(2,1)} %all-to-all-done.in_ref), custom_call_target="tpu_custom_call" | custom-call | tf_op jit(solution)/shard_map/predict/pallas_call | solution.py:289
  181.6 6.0 %all-to-all-start.1 = ((bf16[32,600,128]{2,1,0:T(8,128)(2,1)}), bf16[32,600,128]{2,1,0:T(8,128)(2,1)}, u32[]{:S(2)}, u32[]{:S(2)}) async-start(bf16[32,600,128]{2,1,0:T(8,128)(2,1)} %predict.1), calls=%async_computation.1 | async-start | bytes 9830400 | tf_op jit(solution)/shard_map/all_to_all | solution.py:328
  187.6 0.8 fusion.1.table_ref
  188.4 109.4 %all-to-all-done.1 = bf16[32,600,128]{2,1,0:T(8,128)(2,1)} async-done(((bf16[32,600,128]{2,1,0:T(8,128)(2,1)}), bf16[32,600,128]{2,1,0:T(8,128)(2,1)}, u32[]{:S(2)}, u32[]{:S(2)}) %all-to-all-start.1) | async-done | bytes 4915232 | tf_op jit(solution)/shard_map/all_to_all | solution.py:328
  297.8 0.0 copy-start.1
  297.8 27.5 %inverse.1 = bf16[4,20,160,1024]{3,2,1,0:T(8,128)(2,1)} custom-call(bf16[192,1024]{1,0:T(8,128)(2,1)} %fusion.1.table_ref, bf16[19200,128]{1,0:T(8,128)(2,1)} %bitcast.8.matched_ref, bf16[4,20,160,1024]{3,2,1,0:T(8,128)(2,1)} %bitcast.25), custom_call_target="tpu_custom_call" | custom-call | tf_op jit(solution)/shard_map/inverse/pallas_call | solution.py:173
  325.3 0.0 copy-done.1
  (11 shorter events, 0.1 us)
Async XLA Ops:
  0.0 28.5 %copy-start = (f32[16,7,64]{2,0,1:T(8,128)S(1)}, f32[16,7,64]{2,0,1:T(8,128)}, u32[]{:S(2)}) copy-start(f32[16,7,64]{2,0,1:T(8,128)} %param.3) | copy-start | bytes 86020
  21.0 117.6 %all-to-all-start = ((bf16[32,600,128]{2,1,0:T(8,128)(2,1)}), bf16[32,600,128]{2,1,0:T(8,128)(2,1)}, u32[]{:S(2)}, u32[]{:S(2)}) async-start(bf16[32,600,128]{2,1,0:T(8,128)(2,1)} %bitcast.26), calls=%async_computation | async-start | bytes 9830400 | tf_op jit(solution)/shard_map/all_to_all | solution.py:323
  181.6 116.2 %all-to-all-start.1 = ((bf16[32,600,128]{2,1,0:T(8,128)(2,1)}), bf16[32,600,128]{2,1,0:T(8,128)(2,1)}, u32[]{:S(2)}, u32[]{:S(2)}) async-start(bf16[32,600,128]{2,1,0:T(8,128)(2,1)} %predict.1), calls=%async_computation.1 | async-start | bytes 9830400 | tf_op jit(solution)/shard_map/all_to_all | solution.py:328
  297.8 27.5 %copy-start.1 = (f32[16,7,64]{2,0,1:T(8,128)S(1)}, f32[16,7,64]{2,0,1:T(8,128)}, u32[]{:S(2)}) copy-start(f32[16,7,64]{2,0,1:T(8,128)} %param.3) | copy-start | bytes 86020

commit v2 on v1

--- a/solution.py
+++ b/solution.py
@@ -17,6 +17,7 @@
 RWIN = 40
 LANES = 128
 AXES = ("panel", "freq")
+MESH = pl.DeviceIdType.MESH
 
 
 def wave_table(freq_bins, sample_index):
@@ -191,115 +192,241 @@
 
 
 def predict_kernel(
-    plan, weight_ref, in_ref, out_ref, left_ref, right_ref, first_ref, side_ref, ahead_ref, fold_ref
+    plan,
+    weight_ref,
+    sent_ref,
+    back_ref,
+    got_ref,
+    out_ref,
+    left_ref,
+    right_ref,
+    first_ref,
+    side_ref,
+    ahead_ref,
+    fold_ref,
+    send_sem,
+    got_sem,
+    own_sem,
+    back_send_sem,
+    back_sem,
+    back_own_sem,
 ):
     shots, group, fold, tail = plan.shots, plan.group, plan.fold, plan.tail
-    side, columns, panels = plan.side, plan.columns, plan.panels
+    side, columns, panels, devices = plan.side, plan.columns, plan.panels, plan.devices
+    rows_of, slices = plan.rows, plan.slices
     scale = jnp.float32(1.0 / math.sqrt(NS))
     tails_at = columns * LANES
-
-    for panel in range(panels):
-        parts = plan.cut(panel * shots, shots)
-        for column in range(columns):
-            source = panel * columns + column
-            for part in range(2):
-                lanes = slice(part * side + column * LANES, part * side + (column + 1) * LANES)
-                for offset, row, length in parts:
-                    at = part * shots + offset
-                    left_ref[row : row + length, lanes] = in_ref[source, at : at + length, :]
-            packed = in_ref[source, 2 * shots :, :].astype(jnp.float32)
-            for part in range(2):
-                for a in range(fold):
-                    side_ref[
-                        part,
-                        panel * shots + a * group : panel * shots + (a + 1) * group,
-                        column * tail : (column + 1) * tail,
-                    ] = packed[part * group : (part + 1) * group, a * tail : (a + 1) * tail]
-    for natural, moved, length in plan.runs:
-        for part in range(2):
-            left_ref[
-                moved : moved + length, part * side + tails_at : (part + 1) * side
-            ] = side_ref[part, natural : natural + length, :].astype(jnp.bfloat16)
+    my_panel, my_column = lax.axis_index("panel"), lax.axis_index("freq")
+    me = my_panel * columns + my_column
+
+    def place_of(device):
+        return {"panel": device // columns, "freq": lax.rem(device, columns)}
+
+    def partner(i):
+        shift = devices // 2 + (1 - 2 * lax.rem(i, 2)) * ((i + 1) // 2)
+        return lax.rem(me + shift, devices)
+
+    barrier = pltpu.get_barrier_semaphore()
+
+    @pl.loop(0, devices - 1)
+    def _(i):
+        pl.semaphore_signal(barrier, inc=1, device_id=place_of(partner(i)), device_id_type=MESH)
+
+    pl.semaphore_wait(barrier, devices - 1)
+
+    def rows_at(f):
+        return pl.ds(pl.multiple_of(f * rows_of, 8), rows_of)
+
+    @pl.loop(0, slices)
+    def _(f):
+        pltpu.make_async_copy(
+            sent_ref.at[me, rows_at(f)], got_ref.at[f, me], own_sem.at[f]
+        ).start()
+
+        @pl.loop(0, devices - 1)
+        def _(i):
+            device = partner(i)
+            pltpu.make_async_remote_copy(
+                src_ref=sent_ref.at[device, rows_at(f)],
+                dst_ref=got_ref.at[f, me],
+                send_sem=send_sem,
+                recv_sem=got_sem.at[f],
+                device_id=place_of(device),
+                device_id_type=MESH,
+            ).start()
+
+    ahead_ref[:RIM, :] = jnp.zeros((RIM, 2 * side), jnp.float32)
+    ahead_ref[RIM + side :, :] = jnp.zeros((RIM, 2 * side), jnp.float32)
 
     def fill(from_ref):
         right_ref[:side, :] = from_ref[...]
         right_ref[side:, :side] = -from_ref[:, side:]
         right_ref[side:, side:] = from_ref[:, :side]
 
-    fill(left_ref)
-
-    @pl.loop(0, 2 * side // CHUNK)
-    def _(k):
-        lanes = pl.ds(pl.multiple_of(k * CHUNK, CHUNK), CHUNK)
-        total = jnp.dot(left_ref[...], right_ref[:, lanes], preferred_element_type=jnp.float32)
-        first_ref[:, lanes] = (total * scale).astype(jnp.bfloat16)
-
-    fill(first_ref)
-    ahead_ref[:RIM, :] = jnp.zeros((RIM, 2 * side), jnp.float32)
-    ahead_ref[RIM + side :, :] = jnp.zeros((RIM, 2 * side), jnp.float32)
-
-    @pl.loop(0, 2 * side // CHUNK)
-    def _(k):
-        lanes = pl.ds(pl.multiple_of(k * CHUNK, CHUNK), CHUNK)
-        total = jnp.dot(left_ref[...], right_ref[:, lanes], preferred_element_type=jnp.float32)
-        value = first_ref[:, lanes].astype(jnp.float32) - total * scale
-        value = value.astype(jnp.bfloat16).astype(jnp.float32)
+    def panel_at(i):
+        return lax.rem(my_panel + panels // 2 + i, panels)
+
+    def send_back(f, panel):
+        for column in range(columns):
+            device = panel * columns + column
+            own = device == me
+
+            @pl.when(own)
+            def _():
+                pltpu.make_async_copy(
+                    out_ref.at[f, device], back_ref.at[me, rows_at(f)], back_own_sem.at[f]
+                ).start()
+
+            @pl.when(jnp.logical_not(own))
+            def _():
+                pltpu.make_async_remote_copy(
+                    src_ref=out_ref.at[f, device],
+                    dst_ref=back_ref.at[me, rows_at(f)],
+                    send_sem=back_send_sem,
+                    recv_sem=back_sem,
+                    device_id={"panel": panel, "freq": column},
+                    device_id_type=MESH,
+                ).start()
+
+    @pl.loop(0, slices)
+    def _(f):
+        pltpu.make_async_copy(
+            sent_ref.at[me, rows_at(f)], got_ref.at[f, me], own_sem.at[f]
+        ).wait()
+        others = got_ref.at[f, pl.ds(0, devices - 1)]
+        pltpu.make_async_copy(others, others, got_sem.at[f]).wait()
+
+        for panel in range(panels):
+            parts = plan.cut(panel * shots, shots)
+            for column in range(columns):
+                source = panel * columns + column
+                for part in range(2):
+                    lanes = slice(
+                        part * side + column * LANES, part * side + (column + 1) * LANES
+                    )
+                    for offset, row, length in parts:
+                        at = part * shots + offset
+                        left_ref[row : row + length, lanes] = got_ref[
+                            f, source, at : at + length, :
+                        ]
+                packed = got_ref[f, source, 2 * shots :, :].astype(jnp.float32)
+                for part in range(2):
+                    for a in range(fold):
+                        side_ref[
+                            part,
+                            panel * shots + a * group : panel * shots + (a + 1) * group,
+                            column * tail : (column + 1) * tail,
+                        ] = packed[part * group : (part + 1) * group, a * tail : (a + 1) * tail]
         for natural, moved, length in plan.runs:
-            ahead_ref[RIM + natural : RIM + natural + length, lanes] = value[moved : moved + length]
-
-    @pl.loop(0, panels)
-    def _(panel):
-        rows = pl.ds(pl.multiple_of(panel * shots, 8), shots + 2 * RIM)
-        for column in range(columns + 1):
-            at = column * LANES
-            real = ahead_ref[rows, at : at + LANES]
-            imag = ahead_ref[rows, side + at : side + at + LANES]
-            sum_real = sum_imag = None
-            for j in range(SPAN):
-                low = RIM - SPAN // 2 + j
-                part_real, part_imag = real[low : low + shots], imag[low : low + shots]
-                weight_real = weight_ref[0, j : j + 1, at : at + LANES]
-                weight_imag = weight_ref[1, j : j + 1, at : at + LANES]
-                term_real = weight_real * part_real - weight_imag * part_imag
-                term_imag = weight_real * part_imag + weight_imag * part_real
-                sum_real = term_real if j == 0 else sum_real + term_real
-                sum_imag = term_imag if j == 0 else sum_imag + term_imag
-            if column < columns:
-                target = panel * columns + column
-                out_ref[target, :shots, :] = sum_real.astype(jnp.bfloat16)
-                out_ref[target, shots : 2 * shots, :] = sum_imag.astype(jnp.bfloat16)
-                continue
-            for part, total in enumerate((sum_real, sum_imag)):
+            for part in range(2):
+                left_ref[
+                    moved : moved + length, part * side + tails_at : (part + 1) * side
+                ] = side_ref[part, natural : natural + length, :].astype(jnp.bfloat16)
+
+        fill(left_ref)
+
+        @pl.loop(0, 2 * side // CHUNK)
+        def _(k):
+            lanes = pl.ds(pl.multiple_of(k * CHUNK, CHUNK), CHUNK)
+            total = jnp.dot(left_ref[...], right_ref[:, lanes], preferred_element_type=jnp.float32)
+            first_ref[:, lanes] = (total * scale).astype(jnp.bfloat16)
+
+        fill(first_ref)
+
+        @pl.loop(0, 2 * side // CHUNK)
+        def _(k):
+            lanes = pl.ds(pl.multiple_of(k * CHUNK, CHUNK), CHUNK)
+            total = jnp.dot(left_ref[...], right_ref[:, lanes], preferred_element_type=jnp.float32)
+            value = first_ref[:, lanes].astype(jnp.float32) - total * scale
+            value = value.astype(jnp.bfloat16).astype(jnp.float32)
+            for natural, moved, length in plan.runs:
+                ahead_ref[RIM + natural : RIM + natural + length, lanes] = value[
+                    moved : moved + length
+                ]
+
+        @pl.loop(0, panels)
+        def _(i):
+            panel = panel_at(i)
+            rows = pl.ds(pl.multiple_of(panel * shots, 8), shots + 2 * RIM)
+            for column in range(columns + 1):
+                at = column * LANES
+                real = ahead_ref[rows, at : at + LANES]
+                imag = ahead_ref[rows, side + at : side + at + LANES]
+                sum_real = sum_imag = None
+                for j in range(SPAN):
+                    low = RIM - SPAN // 2 + j
+                    part_real, part_imag = real[low : low + shots], imag[low : low + shots]
+                    weight_real = weight_ref[f, 0, j : j + 1, at : at + LANES]
+                    weight_imag = weight_ref[f, 1, j : j + 1, at : at + LANES]
+                    term_real = weight_real * part_real - weight_imag * part_imag
+                    term_imag = weight_real * part_imag + weight_imag * part_real
+                    sum_real = term_real if j == 0 else sum_real + term_real
+                    sum_imag = term_imag if j == 0 else sum_imag + term_imag
+                if column < columns:
+                    target = panel * columns + column
+                    out_ref[f, target, :shots, :] = sum_real.astype(jnp.bfloat16)
+                    out_ref[f, target, shots : 2 * shots, :] = sum_imag.astype(jnp.bfloat16)
+                    continue
+                for part, total in enumerate((sum_real, sum_imag)):
+                    for other in range(columns):
+                        for a in range(fold):
+                            fold_ref[
+                                other,
+                                part * group : (part + 1) * group,
+                                a * tail : (a + 1) * tail,
+                            ] = total[
+                                a * group : (a + 1) * group, other * tail : (other + 1) * tail
+                            ]
                 for other in range(columns):
-                    for a in range(fold):
-                        fold_ref[
-                            other,
-                            part * group : (part + 1) * group,
-                            a * tail : (a + 1) * tail,
-                        ] = total[a * group : (a + 1) * group, other * tail : (other + 1) * tail]
-            for other in range(columns):
-                out_ref[panel * columns + other, 2 * shots :, :] = fold_ref[other].astype(
-                    jnp.bfloat16
-                )
+                    out_ref[f, panel * columns + other, 2 * shots :, :] = fold_ref[other].astype(
+                        jnp.bfloat16
+                    )
+
+            @pl.when(i > 0)
+            def _():
+                send_back(f, panel_at(i - 1))
+
+        send_back(f, panel_at(panels - 1))
+
+    others = sent_ref.at[pl.ds(0, devices - 1)]
+    pltpu.make_async_copy(others, others, send_sem).wait()
+
+    @pl.loop(0, slices)
+    def _(f):
+        pltpu.make_async_copy(
+            out_ref.at[f, me], back_ref.at[me, rows_at(f)], back_own_sem.at[f]
+        ).wait()
+
+    others = back_ref.at[pl.ds(0, devices - 1)]
+    pltpu.make_async_copy(others, others, back_send_sem).wait()
+    pltpu.make_async_copy(others, others, back_sem).wait()
 
 
 def predict(plan, blocks, weights):
     side = plan.side
-    block = pl.BlockSpec((plan.devices, plan.rows, LANES), lambda f: (0, f, 0))
+    held = (plan.slices, plan.devices, plan.rows, LANES)
     return pl.pallas_call(
         functools.partial(predict_kernel, plan),
-        grid=(plan.slices,),
         out_shape=jax.ShapeDtypeStruct(blocks.shape, jnp.bfloat16),
-        in_specs=[pl.BlockSpec((None, 2, 8, side), lambda f: (f, 0, 0, 0)), block],
-        out_specs=block,
+        in_specs=[pl.BlockSpec(memory_space=pltpu.VMEM), pl.BlockSpec(memory_space=pl.ANY)],
+        out_specs=pl.BlockSpec(memory_space=pl.ANY),
         scratch_shapes=[
+            pltpu.VMEM(held, jnp.bfloat16),
+            pltpu.VMEM(held, jnp.bfloat16),
             pltpu.VMEM((side, 2 * side), jnp.bfloat16),
             pltpu.VMEM((2 * side, 2 * side), jnp.bfloat16),
             pltpu.VMEM((side, 2 * side), jnp.bfloat16),
             pltpu.VMEM((2, side, LANES), jnp.float32),
             pltpu.VMEM((side + 2 * RIM, 2 * side), jnp.float32),
             pltpu.VMEM((plan.columns, 2 * plan.group, LANES), jnp.float32),
+            pltpu.SemaphoreType.DMA,
+            pltpu.SemaphoreType.DMA((plan.slices,)),
+            pltpu.SemaphoreType.DMA((plan.slices,)),
+            pltpu.SemaphoreType.DMA,
+            pltpu.SemaphoreType.DMA,
+            pltpu.SemaphoreType.DMA((plan.slices,)),
         ],
+        compiler_params=pltpu.CompilerParams(collective_id=0, has_side_effects=True),
         name="predict",
     )(weights, blocks)
 
@@ -320,12 +447,10 @@
     wire = (plan.devices, plan.slices * plan.rows, LANES)
 
     spectra = spectrum(plan, traces, forward).reshape(wire)
-    received = lax.all_to_all(spectra, AXES, split_axis=0, concat_axis=0, tiled=True)
     own = lax.axis_index(AXES) * plan.slices + jnp.arange(plan.slices, dtype=jnp.int32)
     weights = jnp.stack([moved_lanes(plan, w) for w in response(filters, FLO + own)], axis=1)
     weights = jnp.pad(weights, ((0, 0), (0, 0), (0, 8 - SPAN), (0, 0)))
-    matched = predict(plan, received, weights)
-    returned = lax.all_to_all(matched, AXES, split_axis=0, concat_axis=0, tiled=True)
+    returned = predict(plan, spectra, weights)
     return subtract(plan, traces, returned.reshape(NF * plan.rows, LANES), inverse)
 
 

time: 326 us -> 272 us (0.83)
  waiting for transfers between devices: 217 us -> 0 us
  Pallas kernels: 89 us -> 264 us
  starting transfers between devices: 13.5 us -> 0 us
    all_to_all x2 -> x0, waiting for transfers between devices: 217 us -> none  [the longest x1 109 us: per_device(): lax.all_to_all(matched, AXES, split_axis=0, concat_axis=0, tiled=True)]
    pallas_call x1, Pallas kernels: 42.9 us -> 218 us  [predict(): pl.pallas_call(functools.partial(predict_kernel, plan), out_shape=jax.Sha...]
    all_to_all x2 -> x0, starting transfers between devices: 13.5 us -> none  [the longest x1 7.44 us: per_device(): lax.all_to_all(spectra, AXES, split_axis=0, concat_axis=0, tiled=True)]
  transfers between devices with their start and end apart: 2 -> 0, of which waited for: 2 -> 0; matrix products, arithmetic and copies ran while one was open for 1% -> 0% of each run, Pallas kernels for 0% -> 0%
where the time goes in v2:
time: 272 us; the launch traced here: 271 us
  Pallas kernels  264 us (97%)
  other arithmetic  3.94 us (1%)
    pallas_call x1, Pallas kernels, predict(): pl.pallas_call(functools.partial(predict_kernel, plan), out_shape=jax.Sha...  218 us
    pallas_call x1, Pallas kernels, subtract(): pl.pallas_call(functools.partial(inverse_kernel, plan, step_size), grid=(...  27.5 us
    pallas_call x1, Pallas kernels, spectrum(): pl.pallas_call(functools.partial(spectrum_kernel, plan, step_size), grid=...  18.6 us

profile of v2, /device:TPU:0, one launch (start us, length us, event | category | flops | bytes accessed | tf_op | source)
XLA Modules:
  0.0 270.6 jit_solution(13903703729108024212)
XLA Ops:
  0.0 0.0 copy-start
  0.0 0.8 copy-done
  0.8 0.5 fusion
  1.4 0.5 convolution_bitcast_fusion
  1.9 0.1 broadcast_in_dim.4
  2.1 0.1 reshape_reshape.6
  2.2 0.1 reshape.35
  2.3 0.1 broadcast_in_dim.5
  2.4 0.1 reshape_reshape.7
  2.6 0.1 reshape.37
  2.7 0.7 select_maximum_fusion.weight_ref
  3.4 1.6 fusion.8
  5.0 0.8 multiply_convert_fusion.table_ref
  5.8 0.8 fusion.1.table_ref
  6.7 18.6 %spectrum.1 = bf16[19200,128]{1,0:T(8,128)(2,1)} custom-call(bf16[192,1024]{1,0:T(8,128)(2,1)} %multiply_convert_fusion.table_ref, bf16[4,20,160,1024]{3,2,1,0:T(8,128)(2,1)} %bitcast.24), custom_call_target="tpu_custom_call" | custom-call | tf_op jit(solution)/shard_map/spectrum/pallas_call | solution.py:116
  25.2 217.9 %predict.1 = bf16[32,600,128]{2,1,0:T(8,128)(2,1)} custom-call(f32[3,2,8,640]{3,2,1,0:T(8,128)} %select_maximum_fusion.weight_ref, bf16[32,600,128]{2,1,0:T(8,128)(2,1)} %bitcast.27), custom_call_target="tpu_custom_call" | custom-call | tf_op jit(solution)/shard_map/predict/pallas_call | solution.py:408
  243.1 27.5 %inverse.1 = bf16[4,20,160,1024]{3,2,1,0:T(8,128)(2,1)} custom-call(bf16[192,1024]{1,0:T(8,128)(2,1)} %fusion.1.table_ref, bf16[19200,128]{1,0:T(8,128)(2,1)} %bitcast.26, bf16[4,20,160,1024]{3,2,1,0:T(8,128)(2,1)} %bitcast.25), custom_call_target="tpu_custom_call" | custom-call | tf_op jit(solution)/shard_map/inverse/pallas_call | solution.py:174
  (11 shorter events, 0.1 us)
Async XLA Ops:
  0.0 0.8 copy-start
